TPU v7x, 32 devices: a whole 2x2x4 slice. The times are simulated.
32 devices in a mesh: member: 4 (over y, core), space: 8 (over z, x).
Axes of the slice: x: 2, y: 2, z: 4, core: 2. Of those that a mesh axis runs over, the one named last changes fastest.
Arguments:
- prior_sample: float32 [256, 65536], P('member', 'space'), may hold values from -6 to 6
- measured_point_location: int32 [32, 128], P('space'), may hold values from 0 to 8191
- measured_data: float32 [32, 128], P('space'), may hold values from -12 to 12
- measurement_noise_sigma: float32 [32, 128], P('space'), may hold values from 2 to 64
- measured_slots_used: int32 [8], P('space'), may hold values from 128 to 512, as said below
Outputs:
- analysis: float32 [256, 65536], P('member', 'space')
Inputs may be any that keep to these rules, and one draw needn't show every extreme that they name: measured_slots_used gives for each space block how many of its first slots are in use; some block uses all 512 slots. `measured_point_location`: each index is a state point of the observation's own space block.
All inputs are finite; a program needn't handle non-finite values.
Results may differ from a plain program's by a relative error of at most 0.000088.
Values sent between devices are 32-bit elements; how exact they have to be, the bound alone decides.
A program may use at most 64 MiB of HBM per device.

v0:
```python
import functools
import math

import jax
import jax.numpy as jnp
from jax import lax
from jax.experimental import pallas as pl
from jax.experimental.pallas import tpu as pltpu
from jax.sharding import PartitionSpec as P


def solve_lower(lower_factor, target):
    return lax.linalg.triangular_solve(lower_factor, target, left_side=True, lower=True)


def general_body(
    prior_sample,
    measured_point_location,
    measured_data,
    measurement_noise_sigma,
    measured_slots_used,
):
    exact_arithmetic = lax.Precision.HIGHEST
    anomaly_matrix, points_in_region = prior_sample.shape
    region_batches = lax.axis_size("member")
    sample_total = anomaly_matrix * region_batches
    pointwise_spread = points_in_region // region_batches
    linear_position = measured_point_location.reshape(-1)
    obs_blk = linear_position.shape[0]
    observation_deviation = obs_blk // region_batches
    propagated_grid = jnp.take(prior_sample, linear_position, axis=1).reshape(
        anomaly_matrix, region_batches, observation_deviation
    )
    prior_regions = prior_sample.reshape(anomaly_matrix, region_batches, pointwise_spread)
    prior_sample_full, integrate_dynamics = (
        lax.all_to_all(prior_regions, "member", split_axis=1, concat_axis=0, tiled=True),
        lax.all_to_all(propagated_grid, "member", split_axis=1, concat_axis=0, tiled=True),
    )
    integrate_dynamics = integrate_dynamics.reshape(sample_total, observation_deviation)
    rank = lax.axis_index("member")
    start = rank * observation_deviation
    my_value = lax.dynamic_slice_in_dim(measured_data.reshape(-1), start, observation_deviation)
    my_sigma = lax.dynamic_slice_in_dim(
        measurement_noise_sigma.reshape(-1), start, observation_deviation
    )
    slots = start + jnp.arange(observation_deviation, dtype=jnp.int32)
    valid = slots < measured_slots_used[0]
    weight = jnp.where(valid, 1.0 / my_sigma, jnp.zeros_like(my_sigma))
    sim_mean = jnp.mean(integrate_dynamics, axis=0)
    perturbed = (integrate_dynamics - sim_mean[None, :]) * weight[None, :]
    innovation = (my_value - sim_mean) * weight
    gram_loc = jnp.dot(perturbed, perturbed.T, precision=exact_arithmetic)
    cross_loc = jnp.dot(perturbed, innovation, precision=exact_arithmetic)
    gram_block, cross_block = lax.psum((gram_loc, cross_loc), "member")
    gram_all, cross = lax.psum((gram_block, cross_block), "space")
    cov_matrix = gram_all + (sample_total - 1) * jnp.eye(sample_total, dtype=jnp.float32)
    lower_factor = jnp.linalg.cholesky(cov_matrix)
    inverse = solve_lower(lower_factor, jnp.eye(sample_total, dtype=jnp.float32))
    projected = jnp.dot(inverse, cross, precision=exact_arithmetic)
    mean_weight = jnp.dot(inverse.T, projected, precision=exact_arithmetic)
    weight_matrix_update = math.sqrt(sample_total - 1) * inverse + mean_weight[None, :]
    sample_vectors = prior_sample_full.reshape(sample_total, -1)
    prior_average = jnp.mean(sample_vectors, axis=0)
    updated_sample = prior_average[None, :] + jnp.dot(
        weight_matrix_update, sample_vectors - prior_average[None, :], precision=exact_arithmetic
    )
    returned = lax.all_to_all(
        updated_sample.reshape(prior_sample_full.shape),
        "member",
        split_axis=0,
        concat_axis=1,
        tiled=True,
    )
    return returned.reshape(anomaly_matrix, points_in_region)


MESH = pl.DeviceIdType.MESH
VMEM_SPEC = pl.BlockSpec(memory_space=pltpu.VMEM)
LANES = 128
MIB = 1 << 20
SUBLANES = 8


def split2(x):
    high = x.astype(jnp.bfloat16)
    low = (x - high.astype(jnp.float32)).astype(jnp.bfloat16)
    return high, low


def dot3(a, b, dims=((1,), (0,))):
    ah, al = split2(a)
    bh, bl = split2(b)
    d = functools.partial(
        lax.dot_general, dimension_numbers=(dims, ((), ())), preferred_element_type=jnp.float32
    )
    return (d(ah, bl) + d(al, bh)) + d(ah, bh)


def flat_row(ref):
    return jnp.concatenate([ref[i : i + 1, :] for i in range(ref.shape[0])], axis=1)


def gather_kernel(starts, x_ref, idx_ref, out_ref, *chunk_refs):
    step = pl.program_id(0)
    members, points = x_ref.shape
    shape = (SUBLANES, LANES)
    for (first, count), chunk_ref in zip(starts, chunk_refs):

        @pl.when((step >= first) & (step < first + count))
        def _(chunk_ref=chunk_ref):
            chunk_ref[...] = x_ref[...]

    for c in range(idx_ref.shape[0]):
        index = jnp.broadcast_to(idx_ref[c : c + 1, :], shape)
        lane = jnp.bitwise_and(index, LANES - 1)
        block = jnp.right_shift(index, LANES.bit_length() - 1) - step * (points // LANES)
        hits = [block == j for j in range(points // LANES)]
        columns = slice(c * LANES, (c + 1) * LANES)
        for g in range(0, members, SUBLANES):
            old = out_ref[g : g + SUBLANES, columns]
            got = jnp.where(step == 0, jnp.zeros(shape, jnp.float32), old)
            for j in range(points // LANES):
                x = x_ref[g : g + SUBLANES, j * LANES : (j + 1) * LANES]
                got = jnp.where(hits[j], jnp.take_along_axis(x, lane, axis=1), got)
            out_ref[g : g + SUBLANES, columns] = got


def gather_observed(prior, index, starts, tile):
    members, points = prior.shape
    slots = index.size
    f32 = jnp.float32
    return pl.pallas_call(
        functools.partial(gather_kernel, starts),
        grid=(points // tile,),
        out_shape=[jax.ShapeDtypeStruct((members, slots), f32)]
        + [jax.ShapeDtypeStruct((members, count * tile), f32) for _, count in starts],
        in_specs=[
            pl.BlockSpec((members, tile), lambda i: (0, i)),
            pl.BlockSpec(index.shape, lambda i: (0, 0)),
        ],
        out_specs=[pl.BlockSpec((members, slots), lambda i: (0, 0))]
        + [
            pl.BlockSpec(
                (members, tile),
                lambda i, first=first, count=count: (0, jnp.clip(i - first, 0, count - 1)),
            )
            for first, count in starts
        ],
        compiler_params=pltpu.CompilerParams(vmem_limit_bytes=12 * MIB),
        cost_estimate=pl.CostEstimate(
            flops=2 * members * slots * 256, bytes_accessed=16_000_000, transcendentals=0
        ),
    )(prior, index)


def send(src, dst, ssem, rsem, member, space):
    copy = pltpu.make_async_remote_copy(
        src_ref=src,
        dst_ref=dst,
        send_sem=ssem,
        recv_sem=rsem,
        device_id={"member": member, "space": space},
        device_id_type=MESH,
    )
    copy.start()
    return copy


def meet(devices):
    barrier = pltpu.get_barrier_semaphore()
    for member, space in devices:
        pl.semaphore_signal(
            barrier, inc=1, device_id={"member": member, "space": space}, device_id_type=MESH
        )
    pl.semaphore_wait(barrier, len(devices))


def neighbours():
    rank = lax.axis_index("member")
    return rank, rank + 1 - 2 * lax.rem(rank, 2), lax.rem(rank + 2, 4)


def exchange_kernel(ev_ref, out_ref, pair, ssem, rsem):
    rank, _, across = neighbours()
    place = lax.axis_index("space")
    rows = ev_ref.shape[0]
    meet([(across, place)])
    mine = pl.ds(pl.multiple_of((rank // 2) * rows, SUBLANES), rows)
    copy = send(ev_ref, pair.at[mine], ssem, rsem, across, place)
    pair[mine, :] = ev_ref[...]
    copy.wait()
    out_ref[...] = pair[...]


def exchange_observed(ev):
    rows, slots = ev.shape
    dma = pltpu.SemaphoreType.DMA
    pair = (rows * 2, slots)
    return pl.pallas_call(
        exchange_kernel,
        out_shape=jax.ShapeDtypeStruct(pair, jnp.float32),
        in_specs=[VMEM_SPEC],
        out_specs=VMEM_SPEC,
        scratch_shapes=[pltpu.VMEM(pair, jnp.float32), dma(()), dma(())],
        compiler_params=pltpu.CompilerParams(
            collective_id=0, has_side_effects=True, vmem_limit_bytes=4 * MIB
        ),
        cost_estimate=pl.CostEstimate(
            flops=1_000_000, bytes_accessed=20_000_000, transcendentals=0
        ),
    )(ev)


def gram_kernel(
    spaces,
    ev_ref,
    data_ref,
    sigma_ref,
    used_ref,
    out_ref,
    full,
    gram,
    parts,
    total,
    rs_send,
    rs_recv,
    ag_send,
    ag_recv,
    fin_send,
    fin_recv,
    ex_send,
    ex_recv,
):
    rank, side, _ = neighbours()
    place = lax.axis_index("space")
    half = lax.rem(rank, 2)
    samples, slots = full.shape
    rows = samples // 2
    group = samples // 4
    chunk = rows // spaces
    meet([(side, place)] + [(rank, lax.rem(place + d, spaces)) for d in range(1, spaces)])

    shared = []
    for i in range(2):
        source = ev_ref.at[pl.ds(i * group, group)]
        target = full.at[pl.ds(pl.multiple_of((half + 2 * i) * group, SUBLANES), group)]
        shared.append(send(source, target, ex_send.at[i], ex_recv.at[i], side, place))
    for i in range(2):
        own = pl.ds(pl.multiple_of((half + 2 * i) * group, SUBLANES), group)
        full[own, :] = ev_ref[i * group : (i + 1) * group, :]
    slot = lax.broadcasted_iota(jnp.int32, (1, slots), 1)
    weight = jnp.where(slot < used_ref[0], 1.0 / flat_row(sigma_ref), 0.0)
    for copy in shared:
        copy.wait_recv()
    ev = full[...]
    mean = jnp.sum(ev, axis=0, keepdims=True) * (1.0 / samples)
    anomalies = (ev - mean) * weight
    innovation = (flat_row(data_ref) - mean) * weight
    first = lax.broadcasted_iota(jnp.int32, (LANES, slots), 0) == 0
    extra = jnp.where(first, jnp.broadcast_to(innovation, (LANES, slots)), 0.0)
    mine = (full[pl.ds(pl.multiple_of(half * rows, SUBLANES), rows), :] - mean) * weight
    right = jnp.concatenate([anomalies, extra], axis=0)
    gram[...] = dot3(mine, right, ((1,), (1,)))

    copies = []
    for d in range(1, spaces):
        other = lax.rem(place + d, spaces)
        copies.append(
            send(
                gram.at[pl.ds(pl.multiple_of(other * chunk, SUBLANES), chunk)],
                parts.at[d - 1],
                rs_send.at[d - 1],
                rs_recv.at[d - 1],
                rank,
                other,
            )
        )
    acc = gram[pl.ds(pl.multiple_of(place * chunk, SUBLANES), chunk), :]
    for d in range(1, spaces):
        copies[d - 1].wait_recv()
        acc = acc + parts[d - 1]
    piece = pl.ds(pl.multiple_of(half * rows + place * chunk, SUBLANES), chunk)
    total[piece, :] = acc
    spread = []
    for d in range(1, spaces):
        other = lax.rem(place + d, spaces)
        spread.append(
            send(
                total.at[piece], total.at[piece], ag_send.at[d - 1], ag_recv.at[d - 1], rank, other
            )
        )
    for copy in spread:
        copy.wait_recv()
    mine_rows = total.at[pl.ds(pl.multiple_of(half * rows, SUBLANES), rows)]
    last = send(mine_rows, mine_rows, fin_send, fin_recv, side, place)
    last.wait_recv()
    for copy in (*shared, *copies, *spread, last):
        copy.wait_send()
    out_ref[...] = total[...]


def summed_gram(ev, data, sigma, used, spaces):
    rows, slots = ev.shape
    samples = rows * 2
    width = samples + LANES
    dma = pltpu.SemaphoreType.DMA
    return pl.pallas_call(
        functools.partial(gram_kernel, spaces),
        out_shape=jax.ShapeDtypeStruct((samples, width), jnp.float32),
        in_specs=[VMEM_SPEC] * 3 + [pl.BlockSpec(memory_space=pltpu.SMEM)],
        out_specs=VMEM_SPEC,
        scratch_shapes=[
            pltpu.VMEM((samples, slots), jnp.float32),
            pltpu.VMEM((rows, width), jnp.float32),
            pltpu.VMEM((spaces - 1, rows // spaces, width), jnp.float32),
            pltpu.VMEM((samples, width), jnp.float32),
            dma((spaces - 1,)),
            dma((spaces - 1,)),
            dma((spaces - 1,)),
            dma((spaces - 1,)),
            dma(()),
            dma(()),
            dma((2,)),
            dma((2,)),
        ],
        compiler_params=pltpu.CompilerParams(collective_id=1, has_side_effects=True, vmem_limit_bytes=16 * MIB),
        cost_estimate=pl.CostEstimate(
            flops=4_000_000, bytes_accessed=6_000_000, transcendentals=0
        ),
    )(ev, data, sigma, used)


PIVOTS = 4


def inverse_factor(a):
    size = a.shape[0]
    count = size // SUBLANES
    shape = (SUBLANES, size)
    m = [a[SUBLANES * i : SUBLANES * (i + 1), :] for i in range(count)]
    diag = [None] * count
    lane = lax.broadcasted_iota(jnp.int32, shape, 1)
    sub = lax.broadcasted_iota(jnp.int32, shape, 0)

    def column(x, k):
        return jnp.broadcast_to(x[:, k : k + 1], shape)

    def row(x, r):
        return jnp.broadcast_to(x[r : r + 1, :], shape)

    for k in range(0, size, PIVOTS):
        t, r = divmod(k, SUBLANES)
        inside = (lane >= k) & (lane < k + PIVOTS)
        cols = [column(m[t], k + q) for q in range(PIVOTS)]
        pivot = {(q, p): row(cols[p], r + q) for p in range(PIVOTS) for q in range(p, PIVOTS)}
        base = [
            jnp.where(inside, jnp.where(lane == k + q, 1.0, 0.0), row(m[t], r + q))
            for q in range(PIVOTS)
        ]
        inverse = []
        for p in range(PIVOTS):
            inverse.append(1.0 / pivot[p, p])
            for q in range(p + 1, PIVOTS):
                factor = pivot[q, p] * inverse[p]
                base[q] = base[q] - factor * base[p]
                for s in range(q, PIVOTS):
                    pivot[s, q] = pivot[s, q] - factor * pivot[s, p]
        for p in range(PIVOTS):
            old = diag[t]
            diag[t] = pivot[p, p] if old is None else jnp.where(sub >= r + p, pivot[p, p], old)
        for i in range(t, count):
            cols_i = cols if i == t else [column(m[i], k + q) for q in range(PIVOTS)]
            cols_i = list(cols_i)
            if i == t:
                unit = jnp.where(lane - k == sub - r, 1.0, 0.0)
                x = jnp.where(inside & (sub >= r), unit, m[i])
            else:
                x = jnp.where(inside, 0.0, m[i])
            for p in range(PIVOTS):
                mult = cols_i[p] * inverse[p]
                if i == t:
                    mult = jnp.where(sub > r + p, mult, 0.0)
                for q in range(p + 1, PIVOTS):
                    cols_i[q] = cols_i[q] - mult * pivot[q, p]
                x = x - mult * base[p]
            m[i] = x
    out = []
    for i in range(count):
        keep = lane <= sub + SUBLANES * i
        out.append(jnp.where(keep, m[i] * lax.rsqrt(diag[i]), 0.0))
    return jnp.concatenate(out, axis=0)


def eye_mask(rows, cols):
    shape = (rows, cols)
    return lax.broadcasted_iota(jnp.int32, shape, 0) == lax.broadcasted_iota(jnp.int32, shape, 1)


def transform_kernel(g_ref, out_ref, inv_ref):
    samples = g_ref.shape[0]
    b = LANES
    ridge = float(samples - 1)
    n = samples // b
    work = {}
    for i in range(n):
        for j in range(i + 1):
            block = g_ref[i * b : (i + 1) * b, j * b : (j + 1) * b]
            work[i, j] = block + jnp.where(eye_mask(b, b), ridge, 0.0) if i == j else block
    inv = {}
    low = {}
    for k in range(n):
        inv[k, k] = inverse_factor(work[k, k])
        for i in range(k + 1, n):
            low[i, k] = dot3(work[i, k], inv[k, k], ((1,), (1,)))
        for i in range(k + 1, n):
            for j in range(k + 1, i + 1):
                work[i, j] = work[i, j] - dot3(low[i, k], low[j, k], ((1,), (1,)))
        for j in range(k):
            acc = dot3(low[k, j], inv[j, j])
            for s in range(j + 1, k):
                acc = acc + dot3(low[k, s], inv[s, j])
            inv[k, j] = -dot3(inv[k, k], acc)
    zero = jnp.zeros((b, b), jnp.float32)
    full = jnp.concatenate(
        [
            jnp.concatenate([inv[i, j] if j <= i else zero for j in range(n)], axis=1)
            for i in range(n)
        ],
        axis=0,
    )
    inv_ref[...] = full
    cross = g_ref[:, samples : samples + b]
    projected = dot3(full, cross)
    mean_weight = jnp.sum(full * projected[:, 0:1], axis=0, keepdims=True)
    out_ref[...] = math.sqrt(samples - 1) * full + mean_weight


def transform_of(gram):
    samples = gram.shape[0]
    return pl.pallas_call(
        transform_kernel,
        out_shape=jax.ShapeDtypeStruct((samples, samples), jnp.float32),
        in_specs=[VMEM_SPEC],
        out_specs=VMEM_SPEC,
        scratch_shapes=[pltpu.VMEM((samples, samples), jnp.float32)],
        compiler_params=pltpu.CompilerParams(vmem_limit_bytes=8 * MIB),
        cost_estimate=pl.CostEstimate(
            flops=4_000_000, bytes_accessed=4_000_000, transcendentals=0
        ),
    )(gram)


def analysis_kernel(t_ref, own_ref, side_ref, across_ref, both_ref, out_ref, x_ref):
    rank = lax.axis_index("member")
    rows = own_ref.shape[0]
    samples = x_ref.shape[0]
    side = rank + 1 - 2 * lax.rem(rank, 2)
    across = lax.rem(rank + 2, 4)
    both = lax.rem(side + 2, 4)
    pieces = ((rank, own_ref), (side, side_ref), (across, across_ref), (both, both_ref))
    total = None
    for member, ref in pieces:
        part = jnp.sum(ref[...], axis=0, keepdims=True)
        total = part if total is None else total + part
    mean = total * (1.0 / samples)
    for member, ref in pieces:
        x_ref[pl.ds(pl.multiple_of(member * rows, SUBLANES), rows), :] = ref[...] - mean
    mine = t_ref[pl.ds(pl.multiple_of(rank * rows, SUBLANES), rows), :]
    th, tl = split2(mine)
    xh, xl = split2(x_ref[...])
    dot = functools.partial(jnp.dot, preferred_element_type=jnp.float32)
    both_parts = dot(jnp.concatenate([th, tl], axis=0), xh)
    out_ref[...] = mean + ((both_parts[rows:] + dot(th, xl)) + both_parts[:rows])


def analysis_chunk(transform, own, pieces, first, out, tile=1024):
    rows, points = own.shape
    samples = transform.shape[0]
    whole = pl.BlockSpec((samples, samples), lambda i: (0, 0))
    placed = pl.BlockSpec((rows, tile), lambda i: (0, i + first))
    block = pl.BlockSpec((rows, tile), lambda i: (0, i))
    kernel, extra, specs, alias = analysis_kernel, (), [], {}
    if out is not None:
        kernel = lambda t, o, s, a, b, _, *rest: analysis_kernel(t, o, s, a, b, *rest)
        extra, specs, alias = (out,), [pl.BlockSpec(memory_space=pl.ANY)], {5: 0}
    return pl.pallas_call(
        kernel,
        grid=(pieces[1].shape[1] // tile,),
        out_shape=jax.ShapeDtypeStruct((rows, points), jnp.float32),
        in_specs=[whole, placed, placed] + [block] * 2 + specs,
        out_specs=placed,
        scratch_shapes=[pltpu.VMEM((samples, tile), jnp.float32)],
        input_output_aliases=alias,
        compiler_params=pltpu.CompilerParams(vmem_limit_bytes=12 * MIB),
    )(transform, own, *pieces, *extra)


TILE = 1024
EIGHTHS = (1, 3, 3, 1)


def body(*arrays):
    prior_sample = arrays[0]
    rows, points = prior_sample.shape
    members, spaces = lax.axis_size("member"), lax.axis_size("space")
    if (
        members != 4
        or rows * members % (2 * SUBLANES * spaces)
        or rows * members % LANES
        or rows % SUBLANES
        or points % (8 * TILE)
    ):
        return general_body(*arrays)
    return fast_body(members, spaces, *arrays)


def fast_body(members, spaces, prior_sample, location, data, sigma, used):
    points = prior_sample.shape[1]
    near = [(i, i ^ 1) for i in range(members)]
    far = [(i, i ^ 2) for i in range(members)]
    counts = [e * points // (8 * TILE) for e in EIGHTHS]
    starts = [(sum(counts[:i]), n) for i, n in enumerate(counts)]
    across = [lax.ppermute(prior_sample[:, : counts[0] * TILE], "member", far)]
    side = lax.ppermute(prior_sample, "member", near)
    observed, *chunks = gather_observed(prior_sample, location, starts[1:], TILE)
    gathered = exchange_observed(observed)
    *chunks, gathered = lax.optimization_barrier((*chunks, gathered))
    for chunk in chunks:
        across.append(lax.ppermute(chunk, "member", far))
    gram = summed_gram(gathered, data, sigma, used, spaces)
    across[0], gram = lax.optimization_barrier((across[0], gram))
    both = lax.ppermute(across[0], "member", near)
    out = transform = transform_of(gram)
    result = None
    for i, (first, _) in enumerate(starts):
        now = both
        if i + 1 < len(starts):
            across[i + 1], out = lax.optimization_barrier((across[i + 1], out))
            if i == 0:
                transform = out
            else:
                result = out
            both = lax.ppermute(across[i + 1], "member", near)
        result = analysis_chunk(
            transform, prior_sample, (side, across[i], now), first, result
        )
        out = result
    return result


def solution(mesh):
    placed = (
        P("member", "space"),
        P("space", None),
        P("space", None),
        P("space", None),
        P("space"),
    )
    return jax.shard_map(
        body, mesh=mesh, in_specs=placed, out_specs=P("member", "space"), check_vma=False
    )
```

profile of v0, /device:TPU:0, one launch (start us, length us, event | category | flops | bytes accessed | tf_op | source)
XLA Modules:
  0.0 81.3 jit_solution(87002444550568553)
XLA Ops:
  0.0 0.5 collective-permute-start.2
  0.5 1.6 %copy-done = f32[64,8192]{1,0:T(8,128)S(1)} copy-done((f32[64,8192]{1,0:T(8,128)S(1)}, f32[64,8192]{1,0:T(8,128)}, u32[]{:S(2)}) %copy-start) | copy-done | bytes 2097176
  2.1 0.7 copy-done.2
  2.8 3.5 %shard_map.55 = (f32[64,512]{1,0:T(8,128)S(1)}, f32[64,3072]{1,0:T(8,128)S(1)}, f32[64,3072]{1,0:T(8,128)S(1)}, f32[64,1024]{1,0:T(8,128)S(1)}) custom-call(f32[64,8192]{1,0:T(8,128)S(1)} %copy-done, s32[4,128]{1,0:T(4,128)S(1)} %copy-done.2), custom_call_target="tpu_custom_call" | custom-call | flops 16777216 | bytes 16000000 | tf_op jit(solution)/shard_map/pallas_call | solution.py:132
  6.3 6.8 %shard_map.56.ev_ref = f32[128,512]{1,0:T(8,128)S(1)} custom-call(f32[64,512]{1,0:T(8,128)S(1)} %get-tuple-element.24.ev_ref), custom_call_target="tpu_custom_call" | custom-call | flops 1000000 | bytes 20000000 | tf_op jit(solution)/shard_map/pallas_call | solution.py:199
  13.0 1.8 %collective-permute-start = (f32[64,3072]{1,0:T(8,128)S(1)}, f32[64,3072]{1,0:T(8,128)S(1)}, u32[]{:S(2)}, u32[]{:S(2)}) collective-permute-start(f32[64,3072]{1,0:T(8,128)S(1)} %get-tuple-element.25), channel_id=1, source_target_pairs={{0,16},{8,24},{16,0},{24,8},{1,17},{9,25},{17,1},{25,9},{2,18},{10... | collective-permute-start | bytes 2359304 | tf_op jit(solution)/shard_map/ppermute | solution.py:529
  14.8 0.3 collective-permute-start.5
  15.1 1.8 %collective-permute-start.1 = (f32[64,1024]{1,0:T(8,128)S(1)}, f32[64,1024]{1,0:T(8,128)S(1)}, u32[]{:S(2)}, u32[]{:S(2)}) collective-permute-start(f32[64,1024]{1,0:T(8,128)S(1)} %slice.3), channel_id=1, source_target_pairs={{0,16},{8,24},{16,0},{24,8},{1,17},{9,25},{17,1},{25,9},{2,18},{10... | collective-permute-start | bytes 786440 | tf_op jit(solution)/shard_map/ppermute | solution.py:523
  17.6 17.2 %shard_map.57.g_ref = f32[256,384]{1,0:T(8,128)S(1)} custom-call(f32[128,512]{1,0:T(8,128)S(1)} %shard_map.56.ev_ref, f32[4,128]{1,0:T(4,128)S(1)} %copy-done.3, f32[4,128]{1,0:T(4,128)S(1)} %copy-done.4, s32[1]{0:T(128)S(6)} %copy.12.used_ref), custom_call_target="tpu_custom_call" | custom-call | flops 4000000 | bytes 6000000 | tf_op jit(solution)/shard_map/pallas_call | solution.py:307
  34.9 20.1 %collective-permute-done.1.across_ref = f32[64,1024]{1,0:T(8,128)S(1)} collective-permute-done((f32[64,1024]{1,0:T(8,128)S(1)}, f32[64,1024]{1,0:T(8,128)S(1)}, u32[]{:S(2)}, u32[]{:S(2)}) %collective-permute-start.1) | collective-permute-done | bytes 262176 | tf_op jit(solution)/shard_map/ppermute | solution.py:523
  54.9 12.0 %shard_map.58.t_ref.t = f32[256,256]{1,0:T(8,128)S(1)} custom-call(f32[256,384]{1,0:T(8,128)S(1)} %shard_map.57.g_ref), custom_call_target="tpu_custom_call" | custom-call | flops 4000000 | bytes 4000000 | tf_op jit(solution)/shard_map/pallas_call | solution.py:440
  67.0 0.6 collective-permute-start.4
  67.6 0.0 collective-permute-done.6.both_ref
  67.6 0.0 collective-permute-done.2.side_ref.s
  67.6 1.2 %shard_map.59._ = f32[64,8192]{1,0:T(8,128)} custom-call(f32[256,256]{1,0:T(8,128)S(1)} %shard_map.58.t_ref.t, f32[64,8192]{1,0:T(8,128)S(1)} %copy-done.1, f32[64,8192]{1,0:T(8,128)S(1)} %collective-permute-done.2.side_ref.s, f32[64,1024]{1,0:T(8,128)S(1)} %collective-permute-done.1.across_ref, f32[64,1024]{1,0:T(8,128)S(1)} %collective-permute-done.6.both_ref), custom_call_target="tpu_custom_call" | custom-call | tf_op jit(solution)/shard_map/pallas_call | solution.py:486
  68.8 0.0 collective-permute-done.5.a
  68.8 0.0 collective-permute-start.8
  68.8 1.5 %collective-permute-start.3 = (f32[64,1024]{1,0:T(8,128)S(1)}, f32[64,1024]{1,0:T(8,128)S(1)}, u32[]{:S(2)}, u32[]{:S(2)}) collective-permute-start(f32[64,1024]{1,0:T(8,128)S(1)} %get-tuple-element.29), channel_id=1, source_target_pairs={{0,16},{8,24},{16,0},{24,8},{1,17},{9,25},{17,1},{25,9},{2,18},{10... | collective-permute-start | bytes 786440 | tf_op jit(solution)/shard_map/ppermute | solution.py:529
  70.3 0.0 collective-permute-done.4.b
  70.3 2.5 %shard_map.60._ = f32[64,8192]{1,0:T(8,128)} custom-call(f32[256,256]{1,0:T(8,128)S(1)} %shard_map.58.t_ref.t, f32[64,8192]{1,0:T(8,128)S(1)} %copy-done.1, f32[64,8192]{1,0:T(8,128)S(1)} %collective-permute-done.2.side_ref.s, f32[64,3072]{1,0:T(8,128)S(1)} %collective-permute-done.a, ...), custom_call_target="tpu_custom_call", output_to_operand_aliasing={{}: (5, {})} | custom-call | tf_op jit(solution)/shard_map/pallas_call | solution.py:486
  72.8 4.7 %collective-permute-done.3.a = f32[64,1024]{1,0:T(8,128)S(1)} collective-permute-done((f32[64,1024]{1,0:T(8,128)S(1)}, f32[64,1024]{1,0:T(8,128)S(1)}, u32[]{:S(2)}, u32[]{:S(2)}) %collective-permute-start.3) | collective-permute-done | bytes 262176 | tf_op jit(solution)/shard_map/ppermute | solution.py:529
  77.5 0.0 collective-permute-done.8.b
  77.5 2.6 %shard_map.61._ = f32[64,8192]{1,0:T(8,128)} custom-call(f32[256,256]{1,0:T(8,128)S(1)} %shard_map.58.t_ref.t, f32[64,8192]{1,0:T(8,128)S(1)} %copy-done.1, f32[64,8192]{1,0:T(8,128)S(1)} %collective-permute-done.2.side_ref.s, f32[64,3072]{1,0:T(8,128)S(1)} %collective-permute-done.5.a, ...), custom_call_target="tpu_custom_call", output_to_operand_aliasing={{}: (5, {})} | custom-call | tf_op jit(solution)/shard_map/pallas_call | solution.py:486
  80.1 1.2 %shard_map.62 = f32[64,8192]{1,0:T(8,128)} custom-call(f32[256,256]{1,0:T(8,128)S(1)} %shard_map.58.t_ref.t, f32[64,8192]{1,0:T(8,128)S(1)} %copy-done.1, f32[64,8192]{1,0:T(8,128)S(1)} %collective-permute-done.2.side_ref.s, f32[64,1024]{1,0:T(8,128)S(1)} %collective-permute-done.3.a, ...), custom_call_target="tpu_custom_call", output_to_operand_aliasing={{}: (5, {})} | custom-call | tf_op jit(solution)/shard_map/pallas_call | solution.py:486
  (13 shorter events, 0.0 us)
Async XLA Ops:
  0.0 67.6 %collective-permute-start.2 = (f32[64,8192]{1,0:T(8,128)}, f32[64,8192]{1,0:T(8,128)S(1)}, u32[]{:S(2)}, u32[]{:S(2)}) collective-permute-start(f32[64,8192]{1,0:T(8,128)} %o.5), channel_id=1, source_target_pairs={{0,8},{8,0},{16,24},{24,16},{1,9},{9,1},{17,25},{25,17},{2,10},{10... | collective-permute-start | bytes 6291464 | tf_op jit(solution)/shard_map/ppermute | solution.py:524
  0.5 1.6 %copy-start = (f32[64,8192]{1,0:T(8,128)S(1)}, f32[64,8192]{1,0:T(8,128)}, u32[]{:S(2)}) copy-start(f32[64,8192]{1,0:T(8,128)} %o.5) | copy-start | bytes 6291460
  2.1 0.7 copy-start.2
  2.8 14.8 %copy-start.3 = (f32[4,128]{1,0:T(4,128)S(1)}, f32[4,128]{1,0:T(4,128)}, u32[]{:S(2)}) copy-start(f32[4,128]{1,0:T(4,128)} %data_ref.1) | copy-start | bytes 6148
  2.8 14.8 %copy-start.4 = (f32[4,128]{1,0:T(4,128)S(1)}, f32[4,128]{1,0:T(4,128)}, u32[]{:S(2)}) copy-start(f32[4,128]{1,0:T(4,128)} %sigma_ref.1) | copy-start | bytes 6148
  2.8 64.8 %copy-start.1 = (f32[64,8192]{1,0:T(8,128)S(1)}, f32[64,8192]{1,0:T(8,128)}, u32[]{:S(2)}) copy-start(f32[64,8192]{1,0:T(8,128)} %o.5) | copy-start | bytes 6291460
  13.0 54.0 %collective-permute-start = (f32[64,3072]{1,0:T(8,128)S(1)}, f32[64,3072]{1,0:T(8,128)S(1)}, u32[]{:S(2)}, u32[]{:S(2)}) collective-permute-start(f32[64,3072]{1,0:T(8,128)S(1)} %get-tuple-element.25), channel_id=1, source_target_pairs={{0,16},{8,24},{16,0},{24,8},{1,17},{9,25},{17,1},{25,9},{2,18},{10... | collective-permute-start | bytes 2359304 | tf_op jit(solution)/shard_map/ppermute | solution.py:529
  14.8 54.0 %collective-permute-start.5 = (f32[64,3072]{1,0:T(8,128)S(1)}, f32[64,3072]{1,0:T(8,128)S(1)}, u32[]{:S(2)}, u32[]{:S(2)}) collective-permute-start(f32[64,3072]{1,0:T(8,128)S(1)} %get-tuple-element.31), channel_id=1, source_target_pairs={{0,16},{8,24},{16,0},{24,8},{1,17},{9,25},{17,1},{25,9},{2,18},{10... | collective-permute-start | bytes 2359304 | tf_op jit(solution)/shard_map/ppermute | solution.py:529
  15.1 39.8 %collective-permute-start.1 = (f32[64,1024]{1,0:T(8,128)S(1)}, f32[64,1024]{1,0:T(8,128)S(1)}, u32[]{:S(2)}, u32[]{:S(2)}) collective-permute-start(f32[64,1024]{1,0:T(8,128)S(1)} %slice.3), channel_id=1, source_target_pairs={{0,16},{8,24},{16,0},{24,8},{1,17},{9,25},{17,1},{25,9},{2,18},{10... | collective-permute-start | bytes 786440 | tf_op jit(solution)/shard_map/ppermute | solution.py:523
  54.9 12.6 %collective-permute-start.6 = (f32[64,1024]{1,0:T(8,128)S(1)}, f32[64,1024]{1,0:T(8,128)S(1)}, u32[]{:S(2)}, u32[]{:S(2)}) collective-permute-start(f32[64,1024]{1,0:T(8,128)S(1)} %collective-permute-done.1.across_ref), channel_id=1, source_target_pairs={{0,8},{8,0},{16,24},{24,16},{1,9},{9,1},{17,25},{25,17},{2,10},{10... | collective-permute-start | bytes 786440 | tf_op jit(solution)/shard_map/ppermute | solution.py:532
  67.0 3.3 %collective-permute-start.4 = (f32[64,3072]{1,0:T(8,128)S(1)}, f32[64,3072]{1,0:T(8,128)S(1)}, u32[]{:S(2)}, u32[]{:S(2)}) collective-permute-start(f32[64,3072]{1,0:T(8,128)S(1)} %collective-permute-done.a), channel_id=1, source_target_pairs={{0,8},{8,0},{16,24},{24,16},{1,9},{9,1},{17,25},{25,17},{2,10},{10... | collective-permute-start | bytes 2359304 | tf_op jit(solution)/shard_map/ppermute | solution.py:543
  68.8 8.7 %collective-permute-start.8 = (f32[64,3072]{1,0:T(8,128)S(1)}, f32[64,3072]{1,0:T(8,128)S(1)}, u32[]{:S(2)}, u32[]{:S(2)}) collective-permute-start(f32[64,3072]{1,0:T(8,128)S(1)} %collective-permute-done.5.a), channel_id=1, source_target_pairs={{0,8},{8,0},{16,24},{24,16},{1,9},{9,1},{17,25},{25,17},{2,10},{10... | collective-permute-start | bytes 2359304 | tf_op jit(solution)/shard_map/ppermute | solution.py:543
  68.8 8.7 %collective-permute-start.3 = (f32[64,1024]{1,0:T(8,128)S(1)}, f32[64,1024]{1,0:T(8,128)S(1)}, u32[]{:S(2)}, u32[]{:S(2)}) collective-permute-start(f32[64,1024]{1,0:T(8,128)S(1)} %get-tuple-element.29), channel_id=1, source_target_pairs={{0,16},{8,24},{16,0},{24,8},{1,17},{9,25},{17,1},{25,9},{2,18},{10... | collective-permute-start | bytes 786440 | tf_op jit(solution)/shard_map/ppermute | solution.py:529
  77.5 2.6 %collective-permute-start.7 = (f32[64,1024]{1,0:T(8,128)S(1)}, f32[64,1024]{1,0:T(8,128)S(1)}, u32[]{:S(2)}, u32[]{:S(2)}) collective-permute-start(f32[64,1024]{1,0:T(8,128)S(1)} %collective-permute-done.3.a), channel_id=1, source_target_pairs={{0,8},{8,0},{16,24},{24,16},{1,9},{9,1},{17,25},{25,17},{2,10},{10... | collective-permute-start | bytes 786440 | tf_op jit(solution)/shard_map/ppermute | solution.py:543
where the time goes:
time: 81.5 us; the launch traced here: 81.3 us
  Pallas kernels  47 us (58%)
  waiting for transfers between devices  24.8 us (30%)
  starting transfers between devices  6.45 us (8%)
  local copies, waits for them, and re-layouts  2.3 us (3%)
    ppermute x1, waiting for transfers between devices, fast_body(): across = [lax.ppermute(prior_sample[:, :counts[0] * TILE], 'member', far)]  20.1 us
    pallas_call x1, Pallas kernels, summed_gram(): pl.pallas_call(functools.partial(gram_kernel, spaces), out_shape=jax.Shap...  17.2 us
    pallas_call x1, Pallas kernels, transform_of(): pl.pallas_call(transform_kernel, out_shape=jax.ShapeDtypeStruct((samples,...  12 us
    pallas_call x4, Pallas kernels, analysis_chunk(): pl.pallas_call(kernel, grid=(pieces[1].shape[1] // tile,), out_shape=jax....  7.5 us
    pallas_call x1, Pallas kernels, exchange_observed(): pl.pallas_call(exchange_kernel, out_shape=jax.ShapeDtypeStruct(pair, jnp....  6.75 us
    ppermute x3, waiting for transfers between devices, fast_body(): across.append(lax.ppermute(chunk, 'member', far))  4.69 us
    ppermute x3, starting transfers between devices, fast_body(): across.append(lax.ppermute(chunk, 'member', far))  3.55 us
    pallas_call x1, Pallas kernels, gather_observed(): pl.pallas_call(functools.partial(gather_kernel, starts), grid=(points //...  3.49 us
  transfers between devices with their start and end apart: 9, of which 2 were waited for; matrix products, arithmetic and copies ran while one was open for 0% of the time, Pallas kernels for 56%

commit v1 on v0

--- a/solution.py
+++ b/solution.py
@@ -94,6 +94,10 @@
         lax.dot_general, dimension_numbers=(dims, ((), ())), preferred_element_type=jnp.float32
     )
     return (d(ah, bl) + d(al, bh)) + d(ah, bh)
+
+
+def in_hbm(x):
+    return pltpu.with_memory_space_constraint(x, pltpu.HBM)
 
 
 def flat_row(ref):
@@ -150,7 +154,7 @@
         cost_estimate=pl.CostEstimate(
             flops=2 * members * slots * 256, bytes_accessed=16_000_000, transcendentals=0
         ),
-    )(prior, index)
+    )(in_hbm(prior), in_hbm(index))
 
 
 def send(src, dst, ssem, rsem, member, space):
@@ -496,7 +500,7 @@
 
 
 TILE = 1024
-EIGHTHS = (1, 3, 3, 1)
+EIGHTHS = (1, 4, 2, 1)
 
 
 def body(*arrays):
@@ -534,7 +538,9 @@
     result = None
     for i, (first, _) in enumerate(starts):
         now = both
-        if i + 1 < len(starts):
+        if 0 < i < len(starts) - 1:
+            both = lax.ppermute(across[i + 1], "member", near)
+        elif i + 1 < len(starts):
             across[i + 1], out = lax.optimization_barrier((across[i + 1], out))
             if i == 0:
                 transform = out

time: 81.5 us -> 73 us (0.90)
  waiting for transfers between devices: 24.8 us -> 14.9 us
  Pallas kernels: 47 us -> 50.9 us
  local copies, waits for them, and re-layouts: 2.3 us -> 0.03 us
    ppermute x1, waiting for transfers between devices: 20.1 us -> 8.31 us  [fast_body(): across = [lax.ppermute(prior_sample[:, :counts[0] * TILE], 'member', far)]]
    pallas_call x1, Pallas kernels: 3.49 us -> 6.08 us  [gather_observed(): pl.pallas_call(functools.partial(gather_kernel, starts), grid=(points //...]
    unnamed x10 -> x6, local copies, waits for them, and re-layouts: 2.28 us -> 0.01 us
    ppermute x3, waiting for transfers between devices: 4.69 us -> 6.56 us  [fast_body(): across.append(lax.ppermute(chunk, 'member', far))]
    ppermute x3, starting transfers between devices: 3.55 us -> 5.27 us  [fast_body(): across.append(lax.ppermute(chunk, 'member', far))]
    pallas_call x1, Pallas kernels: 17.2 us -> 18.8 us  [summed_gram(): pl.pallas_call(functools.partial(gram_kernel, spaces), out_shape=jax.Shap...]
    ppermute x1, starting transfers between devices: 1.8 us -> 0.36 us  [fast_body(): across = [lax.ppermute(prior_sample[:, :counts[0] * TILE], 'member', far)]]
  transfers between devices with their start and end apart: 9 -> 9, of which waited for: 2 -> 2; matrix products, arithmetic and copies ran while one was open for 0% -> 0% of each run, Pallas kernels for 56% -> 51%
where the time goes in v1:
time: 73 us; the launch traced here: 72.8 us
  Pallas kernels  50.9 us (70%)
  waiting for transfers between devices  14.9 us (20%)
  starting transfers between devices  6.19 us (8%)
  between operations  0.74 us (1%)
    pallas_call x1, Pallas kernels, summed_gram(): pl.pallas_call(functools.partial(gram_kernel, spaces), out_shape=jax.Shap...  18.8 us
    pallas_call x1, Pallas kernels, transform_of(): pl.pallas_call(transform_kernel, out_shape=jax.ShapeDtypeStruct((samples,...  12 us
    ppermute x1, waiting for transfers between devices, fast_body(): across = [lax.ppermute(prior_sample[:, :counts[0] * TILE], 'member', far)]  8.31 us
    pallas_call x4, Pallas kernels, analysis_chunk(): pl.pallas_call(kernel, grid=(pieces[1].shape[1] // tile,), out_shape=jax....  7.38 us
    pallas_call x1, Pallas kernels, exchange_observed(): pl.pallas_call(exchange_kernel, out_shape=jax.ShapeDtypeStruct(pair, jnp....  6.59 us
    ppermute x3, waiting for transfers between devices, fast_body(): across.append(lax.ppermute(chunk, 'member', far))  6.56 us
    pallas_call x1, Pallas kernels, gather_observed(): pl.pallas_call(functools.partial(gather_kernel, starts), grid=(points //...  6.08 us
    ppermute x3, starting transfers between devices, fast_body(): across.append(lax.ppermute(chunk, 'member', far))  5.27 us
  transfers between devices with their start and end apart: 9, of which 2 were waited for; matrix products, arithmetic and copies ran while one was open for 0% of the time, Pallas kernels for 51%

profile of v1, /device:TPU:0, one launch (start us, length us, event | category | flops | bytes accessed | tf_op | source)
XLA Modules:
  0.0 72.8 jit_solution(7322052222776955536)
XLA Ops:
  0.0 6.1 %shard_map.55 = (f32[64,512]{1,0:T(8,128)S(1)}, f32[64,4096]{1,0:T(8,128)S(1)}, f32[64,2048]{1,0:T(8,128)S(1)}, f32[64,1024]{1,0:T(8,128)S(1)}) custom-call(f32[64,8192]{1,0:T(8,128)} %o.5, s32[4,128]{1,0:T(4,128)} %idx_ref.1), custom_call_target="tpu_custom_call" | custom-call | flops 16777216 | bytes 16000000 | tf_op jit(solution)/shard_map/pallas_call | solution.py:136
  6.1 6.6 %shard_map.56.ev_ref = f32[128,512]{1,0:T(8,128)S(1)} custom-call(f32[64,512]{1,0:T(8,128)S(1)} %get-tuple-element.20.ev_ref), custom_call_target="tpu_custom_call" | custom-call | flops 1000000 | bytes 20000000 | tf_op jit(solution)/shard_map/pallas_call | solution.py:203
  12.7 1.8 %collective-permute-start = (f32[64,4096]{1,0:T(8,128)S(1)}, f32[64,4096]{1,0:T(8,128)S(1)}, u32[]{:S(2)}, u32[]{:S(2)}) collective-permute-start(f32[64,4096]{1,0:T(8,128)S(1)} %get-tuple-element.21), channel_id=1, source_target_pairs={{0,16},{8,24},{16,0},{24,8},{1,17},{9,25},{17,1},{25,9},{2,18},{10... | collective-permute-start | bytes 3145736 | tf_op jit(solution)/shard_map/ppermute | solution.py:533
  14.5 0.0 collective-permute-start.2
  14.5 0.4 collective-permute-start.1
  14.9 1.7 %collective-permute-start.5 = (f32[64,2048]{1,0:T(8,128)S(1)}, f32[64,2048]{1,0:T(8,128)S(1)}, u32[]{:S(2)}, u32[]{:S(2)}) collective-permute-start(f32[64,2048]{1,0:T(8,128)S(1)} %get-tuple-element.26), channel_id=1, source_target_pairs={{0,16},{8,24},{16,0},{24,8},{1,17},{9,25},{17,1},{25,9},{2,18},{10... | collective-permute-start | bytes 1572872 | tf_op jit(solution)/shard_map/ppermute | solution.py:533
  17.3 18.8 %shard_map.57.g_ref = f32[256,384]{1,0:T(8,128)S(1)} custom-call(f32[128,512]{1,0:T(8,128)S(1)} %shard_map.56.ev_ref, f32[4,128]{1,0:T(4,128)S(1)} %copy-done.1, f32[4,128]{1,0:T(4,128)S(1)} %copy-done.2, s32[1]{0:T(128)S(6)} %copy.12.used_ref), custom_call_target="tpu_custom_call" | custom-call | flops 4000000 | bytes 6000000 | tf_op jit(solution)/shard_map/pallas_call | solution.py:311
  36.1 8.3 %collective-permute-done.1.across_ref = f32[64,1024]{1,0:T(8,128)S(1)} collective-permute-done((f32[64,1024]{1,0:T(8,128)S(1)}, f32[64,1024]{1,0:T(8,128)S(1)}, u32[]{:S(2)}, u32[]{:S(2)}) %collective-permute-start.1) | collective-permute-done | bytes 262176 | tf_op jit(solution)/shard_map/ppermute | solution.py:527
  44.4 12.0 %shard_map.58.t_ref.t = f32[256,256]{1,0:T(8,128)S(1)} custom-call(f32[256,384]{1,0:T(8,128)S(1)} %shard_map.57.g_ref), custom_call_target="tpu_custom_call" | custom-call | flops 4000000 | bytes 4000000 | tf_op jit(solution)/shard_map/pallas_call | solution.py:444
  56.5 0.0 collective-permute-done.a
  56.5 0.1 collective-permute-start.7
  56.6 0.0 collective-permute-done.5.a
  56.6 0.5 collective-permute-start.6
  57.1 1.7 %collective-permute-start.3 = (f32[64,1024]{1,0:T(8,128)S(1)}, f32[64,1024]{1,0:T(8,128)S(1)}, u32[]{:S(2)}, u32[]{:S(2)}) collective-permute-start(f32[64,1024]{1,0:T(8,128)S(1)} %get-tuple-element.25), channel_id=1, source_target_pairs={{0,16},{8,24},{16,0},{24,8},{1,17},{9,25},{17,1},{25,9},{2,18},{10... | collective-permute-start | bytes 786440 | tf_op jit(solution)/shard_map/ppermute | solution.py:533
  58.8 0.0 collective-permute-start.8
  58.8 6.6 %collective-permute-done.3.a = f32[64,1024]{1,0:T(8,128)S(1)} collective-permute-done((f32[64,1024]{1,0:T(8,128)S(1)}, f32[64,1024]{1,0:T(8,128)S(1)}, u32[]{:S(2)}, u32[]{:S(2)}) %collective-permute-start.3) | collective-permute-done | bytes 262176 | tf_op jit(solution)/shard_map/ppermute | solution.py:533
  65.4 0.0 collective-permute-start.4
  65.4 0.0 collective-permute-done.8.both_ref
  65.4 0.0 collective-permute-done.2.side_ref.s
  65.4 1.2 %shard_map.59._ = f32[64,8192]{1,0:T(8,128)} custom-call(f32[256,256]{1,0:T(8,128)S(1)} %shard_map.58.t_ref.t, f32[64,8192]{1,0:T(8,128)S(1)} %copy-done, f32[64,8192]{1,0:T(8,128)S(1)} %collective-permute-done.2.side_ref.s, f32[64,1024]{1,0:T(8,128)S(1)} %collective-permute-done.1.across_ref, f32[64,1024]{1,0:T(8,128)S(1)} %collective-permute-done.8.both_ref), custom_call_target="tpu_custom_call" | custom-call | tf_op jit(solution)/shard_map/pallas_call | solution.py:490
  66.6 3.1 %shard_map.60._ = f32[64,8192]{1,0:T(8,128)} custom-call(f32[256,256]{1,0:T(8,128)S(1)} %shard_map.58.t_ref.t, f32[64,8192]{1,0:T(8,128)S(1)} %copy-done, f32[64,8192]{1,0:T(8,128)S(1)} %collective-permute-done.2.side_ref.s, f32[64,4096]{1,0:T(8,128)S(1)} %collective-permute-done.a, ...), custom_call_target="tpu_custom_call", output_to_operand_aliasing={{}: (5, {})} | custom-call | tf_op jit(solution)/shard_map/pallas_call | solution.py:490
  69.7 0.0 collective-permute-done.6.b
  69.7 1.9 %shard_map.61._ = f32[64,8192]{1,0:T(8,128)} custom-call(f32[256,256]{1,0:T(8,128)S(1)} %shard_map.58.t_ref.t, f32[64,8192]{1,0:T(8,128)S(1)} %copy-done, f32[64,8192]{1,0:T(8,128)S(1)} %collective-permute-done.2.side_ref.s, f32[64,2048]{1,0:T(8,128)S(1)} %collective-permute-done.5.a, ...), custom_call_target="tpu_custom_call", output_to_operand_aliasing={{}: (5, {})} | custom-call | tf_op jit(solution)/shard_map/pallas_call | solution.py:490
  71.6 1.2 %shard_map.62 = f32[64,8192]{1,0:T(8,128)} custom-call(f32[256,256]{1,0:T(8,128)S(1)} %shard_map.58.t_ref.t, f32[64,8192]{1,0:T(8,128)S(1)} %copy-done, f32[64,8192]{1,0:T(8,128)S(1)} %collective-permute-done.2.side_ref.s, f32[64,1024]{1,0:T(8,128)S(1)} %collective-permute-done.3.a, ...), custom_call_target="tpu_custom_call", output_to_operand_aliasing={{}: (5, {})} | custom-call | tf_op jit(solution)/shard_map/pallas_call | solution.py:490
  (9 shorter events, 0.0 us)
Async XLA Ops:
  0.0 14.5 %copy-start = (f32[64,8192]{1,0:T(8,128)S(1)}, f32[64,8192]{1,0:T(8,128)}, u32[]{:S(2)}) copy-start(f32[64,8192]{1,0:T(8,128)} %o.5) | copy-start | bytes 6291460
  0.0 17.3 %copy-start.1 = (f32[4,128]{1,0:T(4,128)S(1)}, f32[4,128]{1,0:T(4,128)}, u32[]{:S(2)}) copy-start(f32[4,128]{1,0:T(4,128)} %data_ref.1) | copy-start | bytes 6148
  0.0 17.3 %copy-start.2 = (f32[4,128]{1,0:T(4,128)S(1)}, f32[4,128]{1,0:T(4,128)}, u32[]{:S(2)}) copy-start(f32[4,128]{1,0:T(4,128)} %sigma_ref.1) | copy-start | bytes 6148
  12.7 43.8 %collective-permute-start = (f32[64,4096]{1,0:T(8,128)S(1)}, f32[64,4096]{1,0:T(8,128)S(1)}, u32[]{:S(2)}, u32[]{:S(2)}) collective-permute-start(f32[64,4096]{1,0:T(8,128)S(1)} %get-tuple-element.21), channel_id=1, source_target_pairs={{0,16},{8,24},{16,0},{24,8},{1,17},{9,25},{17,1},{25,9},{2,18},{10... | collective-permute-start | bytes 3145736 | tf_op jit(solution)/shard_map/ppermute | solution.py:533
  14.5 50.9 %collective-permute-start.2 = (f32[64,8192]{1,0:T(8,128)S(1)}, f32[64,8192]{1,0:T(8,128)S(1)}, u32[]{:S(2)}, u32[]{:S(2)}) collective-permute-start(f32[64,8192]{1,0:T(8,128)S(1)} %copy-done), channel_id=1, source_target_pairs={{0,8},{8,0},{16,24},{24,16},{1,9},{9,1},{17,25},{25,17},{2,10},{10... | collective-permute-start | bytes 6291464 | tf_op jit(solution)/shard_map/ppermute | solution.py:528
  14.5 29.9 %collective-permute-start.1 = (f32[64,1024]{1,0:T(8,128)S(1)}, f32[64,1024]{1,0:T(8,128)S(1)}, u32[]{:S(2)}, u32[]{:S(2)}) collective-permute-start(f32[64,1024]{1,0:T(8,128)S(1)} %slice.3), channel_id=1, source_target_pairs={{0,16},{8,24},{16,0},{24,8},{1,17},{9,25},{17,1},{25,9},{2,18},{10... | collective-permute-start | bytes 786440 | tf_op jit(solution)/shard_map/ppermute | solution.py:527
  14.9 41.7 %collective-permute-start.5 = (f32[64,2048]{1,0:T(8,128)S(1)}, f32[64,2048]{1,0:T(8,128)S(1)}, u32[]{:S(2)}, u32[]{:S(2)}) collective-permute-start(f32[64,2048]{1,0:T(8,128)S(1)} %get-tuple-element.26), channel_id=1, source_target_pairs={{0,16},{8,24},{16,0},{24,8},{1,17},{9,25},{17,1},{25,9},{2,18},{10... | collective-permute-start | bytes 1572872 | tf_op jit(solution)/shard_map/ppermute | solution.py:533
  56.5 10.1 %collective-permute-start.7 = (f32[64,4096]{1,0:T(8,128)S(1)}, f32[64,4096]{1,0:T(8,128)S(1)}, u32[]{:S(2)}, u32[]{:S(2)}) collective-permute-start(f32[64,4096]{1,0:T(8,128)S(1)} %collective-permute-done.a), channel_id=1, source_target_pairs={{0,8},{8,0},{16,24},{24,16},{1,9},{9,1},{17,25},{25,17},{2,10},{10... | collective-permute-start | bytes 3145736 | tf_op jit(solution)/shard_map/ppermute | solution.py:549
  56.6 13.1 %collective-permute-start.6 = (f32[64,2048]{1,0:T(8,128)S(1)}, f32[64,2048]{1,0:T(8,128)S(1)}, u32[]{:S(2)}, u32[]{:S(2)}) collective-permute-start(f32[64,2048]{1,0:T(8,128)S(1)} %collective-permute-done.5.a), channel_id=1, source_target_pairs={{0,8},{8,0},{16,24},{24,16},{1,9},{9,1},{17,25},{25,17},{2,10},{10... | collective-permute-start | bytes 1572872 | tf_op jit(solution)/shard_map/ppermute | solution.py:542
  57.1 8.3 %collective-permute-start.3 = (f32[64,1024]{1,0:T(8,128)S(1)}, f32[64,1024]{1,0:T(8,128)S(1)}, u32[]{:S(2)}, u32[]{:S(2)}) collective-permute-start(f32[64,1024]{1,0:T(8,128)S(1)} %get-tuple-element.25), channel_id=1, source_target_pairs={{0,16},{8,24},{16,0},{24,8},{1,17},{9,25},{17,1},{25,9},{2,18},{10... | collective-permute-start | bytes 786440 | tf_op jit(solution)/shard_map/ppermute | solution.py:533
  58.8 6.6 %collective-permute-start.8 = (f32[64,1024]{1,0:T(8,128)S(1)}, f32[64,1024]{1,0:T(8,128)S(1)}, u32[]{:S(2)}, u32[]{:S(2)}) collective-permute-start(f32[64,1024]{1,0:T(8,128)S(1)} %collective-permute-done.1.across_ref), channel_id=1, source_target_pairs={{0,8},{8,0},{16,24},{24,16},{1,9},{9,1},{17,25},{25,17},{2,10},{10... | collective-permute-start | bytes 786440 | tf_op jit(solution)/shard_map/ppermute | solution.py:536
  65.4 6.2 %collective-permute-start.4 = (f32[64,1024]{1,0:T(8,128)S(1)}, f32[64,1024]{1,0:T(8,128)S(1)}, u32[]{:S(2)}, u32[]{:S(2)}) collective-permute-start(f32[64,1024]{1,0:T(8,128)S(1)} %collective-permute-done.3.a), channel_id=1, source_target_pairs={{0,8},{8,0},{16,24},{24,16},{1,9},{9,1},{17,25},{25,17},{2,10},{10... | collective-permute-start | bytes 786440 | tf_op jit(solution)/shard_map/ppermute | solution.py:542
